TPU v7x, 32 devices: a whole 2x2x4 slice. The times are simulated.
32 devices in a mesh: dp: 8 (over z, y), tp: 4 (over x, core).
Axes of the slice: x: 2, y: 2, z: 4, core: 2. Of those that a mesh axis runs over, the one named last changes fastest.
Arguments:
- inputs: bfloat16 [16384, 2048], P(('dp', 'tp')), may hold values from -6 to 6
- sentence_ids: int32 [32, 512], P(('dp', 'tp')), may hold values from 0 to 3, never falling along the last dimension, each value on 1 to 192 neighbouring positions
- start_states: float32 [128, 2048], P(('dp', 'tp')), may hold values from -5 to 5
- ln_gain: float32 [2048], replicated, may hold values from 0.1 to 1.9
- ln_bias: float32 [2048], replicated, may hold values from -3 to 3
- weight: bfloat16 [6144, 2048], P('tp'), may hold values from -0.125 to 0.125
- gate_bias: float32 [2, 2048], replicated, may hold values from -2 to 4
- out_grad: bfloat16 [16384, 2048], P(('dp', 'tp')), may hold values from -6 to 6
Outputs:
- output: bfloat16 [16384, 2048], P(('dp', 'tp'))
- final_states: float32 [128, 2048], P(('dp', 'tp'))
- input_grad: float32 [16384, 2048], P(('dp', 'tp'))
- weight_grad: float32 [6144, 2048], P('tp')
- gate_bias_grad: float32 [2, 2048], replicated
- ln_gain_grad: float32 [2048], replicated
- ln_bias_grad: float32 [2048], replicated
- start_grad: float32 [128, 2048], P(('dp', 'tp'))
Inputs may be any that keep to these rules, and one draw needn't show every extreme that they name: `sentence_ids`: each row holds the sentence ids of one device's tokens in order: never falling, every id of 0 to 3 present, each sentence 1 to 192 tokens and some sentence exactly 192.
All inputs are finite; a program needn't handle non-finite values.
Results may differ from a plain program's by a relative error of at most 0.006.
Values may be sent and summed in bfloat16 or wider, within the bound.
No kernel may reach another device: no remote copies, remote signals or barrier semaphores. Data moves between devices by JAX's collectives and lax.ppermute only.
A program may use at most 256 MiB of HBM per device.

v0:
```python
import jax
import jax.numpy as jnp
from jax import lax
from jax.sharding import PartitionSpec as P

SENT_DEV = 4


def link(first, second):
    first_decay, first_value = first
    second_decay, second_value = second
    return (first_decay * second_decay, second_decay * first_value + second_value)


def local(inputs, sentence_ids, start_states, ln_gain, ln_bias, weight, gate_bias, out_grad):
    width = inputs.shape[1]
    signal = inputs.astype(jnp.float32)
    centred = signal - jnp.mean(signal, axis=1, keepdims=True)
    rstd = lax.rsqrt(jnp.mean(centred * centred, axis=1, keepdims=True) + 1e-05)
    scaled_in = centred * rstd
    normed = scaled_in * ln_gain + ln_bias
    normed_low = normed.astype(jnp.bfloat16)
    contract_last = (((1,), (1,)), ((), ()))
    contract_first = (((0,), (0,)), ((), ()))
    streams = lax.dot_general(
        normed_low,
        lax.all_gather(weight, "tp", axis=0, tiled=True),
        contract_last,
        preferred_element_type=jnp.float32,
    ).astype(jnp.bfloat16)
    stream_vals = streams.astype(jnp.float32)
    candidate = stream_vals[:, :width]
    forget = jax.nn.sigmoid(stream_vals[:, width : 2 * width] + gate_bias[0])
    reset = jax.nn.sigmoid(stream_vals[:, 2 * width :] + gate_bias[1])
    seg_row = sentence_ids[0]
    first_mask = jnp.concatenate([jnp.ones((1,), bool), seg_row[1:] != seg_row[:-1]])[:, None]
    last_mask = jnp.concatenate([seg_row[:-1] != seg_row[1:], jnp.ones((1,), bool)])[:, None]
    table = (seg_row[:, None] == jnp.arange(SENT_DEV, dtype=jnp.int32)[None, :]).astype(jnp.float32)
    begin = jnp.dot(table, start_states, precision=lax.Precision.HIGHEST)
    zeros_like = jnp.zeros_like(forget)
    decay = jnp.where(first_mask, zeros_like, forget)
    drive = (1.0 - forget) * candidate + jnp.where(first_mask, forget * begin, zeros_like)
    unused, cells = lax.associative_scan(link, (decay, drive), axis=0)
    output = (signal + reset * cells + (1.0 - reset) * normed).astype(jnp.bfloat16)
    picker = table * last_mask.astype(jnp.float32)
    final_states = lax.dot_general(picker, cells, contract_first, precision=lax.Precision.HIGHEST)
    outer = out_grad.astype(jnp.float32)
    shifted = jnp.concatenate([jnp.zeros((1, width), jnp.float32), cells[:-1]], axis=0)
    previous = jnp.where(first_mask, begin, shifted)
    reset_pre_grad = outer * (cells - normed) * reset * (1.0 - reset)
    direct = outer * reset
    next_decay = jnp.concatenate([decay[1:], jnp.zeros((1, width), jnp.float32)], axis=0)
    unused_back, carry_grad = lax.associative_scan(link, (next_decay, direct), reverse=True, axis=0)
    candidate_grad = carry_grad * (1.0 - forget)
    forget_pre_grad = carry_grad * (previous - candidate) * forget * (1.0 - forget)
    start_terms = jnp.where(first_mask, forget * carry_grad, zeros_like)
    start_grad = lax.dot_general(
        table, start_terms, contract_first, precision=lax.Precision.HIGHEST
    )
    stream_grads = jnp.concatenate(
        [candidate_grad, forget_pre_grad, reset_pre_grad], axis=1
    ).astype(jnp.bfloat16)
    bias_part = jnp.stack([jnp.sum(forget_pre_grad, axis=0), jnp.sum(reset_pre_grad, axis=0)])
    columns = stream_grads
    projected_grad = jnp.dot(
        columns,
        lax.all_gather(weight, "tp", axis=0, tiled=True),
        preferred_element_type=jnp.float32,
    )
    columns = stream_grads
    weight_part = lax.psum_scatter(
        lax.dot_general(columns, normed_low, contract_first, preferred_element_type=jnp.float32),
        "tp",
        scatter_dimension=0,
        tiled=True,
    )
    normed_grad = projected_grad + outer * (1.0 - reset)
    gain_part = jnp.sum(normed_grad * scaled_in, axis=0)
    shift_part = jnp.sum(normed_grad, axis=0)
    scaled_grad = normed_grad * ln_gain
    input_grad = (
        rstd
        * (
            scaled_grad
            - jnp.mean(scaled_grad, axis=1, keepdims=True)
            - scaled_in * jnp.mean(scaled_grad * scaled_in, axis=1, keepdims=True)
        )
        + outer
    )
    weight_grad = lax.psum(weight_part, "dp")
    bias_grad, gain_grad, shift_grad = lax.psum((bias_part, gain_part, shift_part), ("dp", "tp"))
    return (
        output,
        final_states,
        input_grad,
        weight_grad,
        bias_grad,
        gain_grad,
        shift_grad,
        start_grad,
    )


def solution(mesh):
    placed = (
        P(("dp", "tp"), None),
        P(("dp", "tp"), None),
        P(("dp", "tp"), None),
        P(),
        P(),
        P("tp", None),
        P(),
        P(("dp", "tp"), None),
    )
    return jax.shard_map(
        local,
        mesh=mesh,
        in_specs=placed,
        out_specs=(
            P(("dp", "tp"), None),
            P(("dp", "tp"), None),
            P(("dp", "tp"), None),
            P("tp", None),
            P(),
            P(),
            P(),
            P(("dp", "tp"), None),
        ),
        check_vma=False,
    )
```

profile of v0, /device:TPU:0, one launch (start us, length us, event | category | flops | bytes accessed | tf_op | source)
XLA Modules:
  0.0 1565.2 jit_solution(1547898737292328093)
XLA Ops:
  10.5 156.7 %all-gather.2.cloned.1.call-done = bf16[6144,2048]{1,0:T(8,128)(2,1)} async-done(((bf16[1536,2048]{1,0:T(8,128)(2,1)}), bf16[6144,2048]{1,0:T(8,128)(2,1)}) %all-gather.2.cloned.1.call-update) | async-done | bytes 25165840 | tf_op jit(solution)/shard_map/all_gather | solution.py:27
  167.2 19.4 %fusion = f32[512,6144]{1,0:T(8,128)} fusion(bf16[6144,2048]{1,0:T(8,128)(2,1)} %all-gather.2.cloned.1.call-done, bf16[512,2048]{1,0:T(8,128)(2,1)S(1)} %copy-done.4, f32[2048]{0:T(1024)S(1)} %copy-done.30, f32[2048]{0:T(1024)S(1)} %copy-done.20, f32[512]{0:T(512)S(1)} %add_rsqrt_fusion, f32[512]{0:T(512)S(1)} %broadcast_multiply_fusion.2), kind=kOutput, calls=%fused_computation.1 | convolution fusion | flops 12897484800 | bytes 39866368 | tf_op jit(solution)/shard_map/dot_general | solution.py:25
  195.2 9.8 slice.477
  205.0 9.8 slice.473
  214.8 10.1 slice.472
  229.8 9.8 slice.549
  239.6 9.8 slice.542
  249.4 9.8 slice.540
  260.1 10.0 slice.537
  270.2 9.8 slice.475
  280.0 9.8 slice.474
  402.9 16.5 %pad.128 = f32[512,2048]{1,0:T(8,128)} pad(f32[256,2048]{1,0:T(8,128)} %pad_maximum_fusion.3, f32[]{:T(128)} %constant.15.clone.1), padding=0_1_1x0_0_0 | pad | bytes 6291460 | tf_op jit(solution)/shard_map/pad | solution.py:43
  419.3 16.6 %pad.129 = f32[512,2048]{1,0:T(8,128)} pad(f32[256,2048]{1,0:T(8,128)} %add.338, f32[]{:T(128)} %constant.15.clone.1), padding=1_0_1x0_0_0 | pad | bytes 6291460 | tf_op jit(solution)/shard_map/pad | solution.py:43
  453.2 9.8 slice.610
  463.1 9.9 slice.546
  472.9 9.8 slice.544
  482.8 16.7 %slice.550 = f32[256,2048]{1,0:T(8,128)} reverse(f32[256,2048]{1,0:T(8,128)} %slice.549), dimensions={0} | reverse | bytes 4194304 | tf_op jit(solution)/shard_map/slice | solution.py:53
  499.4 16.7 %slice.543 = f32[256,2048]{1,0:T(8,128)} reverse(f32[256,2048]{1,0:T(8,128)} %slice.542), dimensions={0} | reverse | bytes 4194304 | tf_op jit(solution)/shard_map/slice | solution.py:53
  516.2 16.6 %slice.545 = f32[256,2048]{1,0:T(8,128)} reverse(f32[256,2048]{1,0:T(8,128)} %slice.544), dimensions={0} | reverse | bytes 4194304 | tf_op jit(solution)/shard_map/slice | solution.py:53
  532.8 16.7 %slice.547 = f32[256,2048]{1,0:T(8,128)} reverse(f32[256,2048]{1,0:T(8,128)} %slice.546), dimensions={0} | reverse | bytes 4194304 | tf_op jit(solution)/shard_map/slice | solution.py:53
  617.8 17.0 %slice.541 = f32[255,2048]{1,0:T(8,128)} reverse(f32[255,2048]{1,0:T(8,128)} %slice.540), dimensions={0} | reverse | bytes 4177920 | tf_op jit(solution)/shard_map/slice | solution.py:53
  634.8 17.1 %slice.611 = f32[255,2048]{1,0:T(8,128)} reverse(f32[255,2048]{1,0:T(8,128)} %slice.610), dimensions={0} | reverse | bytes 4177920 | tf_op jit(solution)/shard_map/slice | solution.py:53
  692.3 16.6 %pad.146 = f32[512,2048]{1,0:T(8,128)} pad(f32[256,2048]{1,0:T(8,128)} %pad_maximum_fusion.4, f32[]{:T(128)} %constant.15.clone.1), padding=0_1_1x0_0_0 | pad | bytes 6291460 | tf_op jit(solution)/shard_map/pad | solution.py:53
  708.9 16.5 %pad.147 = f32[512,2048]{1,0:T(8,128)} pad(f32[256,2048]{1,0:T(8,128)} %add.366, f32[]{:T(128)} %constant.15.clone.1), padding=1_0_1x0_0_0 | pad | bytes 6291460 | tf_op jit(solution)/shard_map/pad | solution.py:53
  732.0 32.6 %rev.2 = f32[512,2048]{1,0:T(8,128)} reverse(f32[512,2048]{1,0:T(8,128)} %add.368), dimensions={0} | reverse | bytes 8388608 | tf_op jit(solution)/shard_map/rev | solution.py:53
  764.7 10.8 fusion.71
  775.5 24.6 %fusion.32 = f32[6144,2048]{1,0:T(8,128)} fusion(bf16[512,2048]{1,0:T(8,128)(2,1)} %get-tuple-element.20, bf16[512,2048]{1,0:T(8,128)(2,1)} %get-tuple-element.18, bf16[512,2048]{1,0:T(8,128)(2,1)} %get-tuple-element.22, bf16[512,2048]{1,0:T(8,128)(2,1)S(1)} %copy-done.4, f32[2048]{0:T(1024)S(1)} %copy-done.32, f32[2048]{0:T(1024)S(1)} %copy-done.20, ...), kind=kOutput, calls=%fused_computation.48 | convolution fusion | flops 12910067712 | bytes 58740736 | tf_op jit(solution)/shard_map/dot_general | solution.py:72
  800.2 346.6 %reduce-scatter.2.cloned.1.call-done = f32[1536,2048]{1,0:T(8,128)} async-done(((f32[6144,2048]{1,0:T(8,128)}), f32[1536,2048]{1,0:T(8,128)}) %reduce-scatter.2.cloned.1.call-update) | async-done | bytes 12582928 | tf_op jit(solution)/shard_map/reduce_scatter | solution.py:71
  1147.6 27.8 %fusion.16 = (f32[2048]{0:T(1024)S(1)}, f32[512]{0:T(512)S(1)}, f32[512]{0:T(512)S(1)}, f32[2048]{0:T(1024)S(1)}, f32[512,2048]{1,0:T(8,128)}) fusion(bf16[512,2048]{1,0:T(8,128)(2,1)S(1)} %copy-done.4, f32[512]{0:T(512)S(1)} %copy-done.28, f32[512]{0:T(512)S(1)} %copy-done.23, f32[2048]{0:T(1024)S(1)} %copy-done.20, f32[2048]{0:T(1024)S(1)} %bitcast.12, ...), kind=kOutput, calls=%fused_computation.25 | convolution fusion | flops 12922646528 | bytes 44081152 | tf_op jit(solution)/shard_map/dot_general | solution.py:65
  1175.4 43.3 %all-reduce.38 = (f32[2,2048]{1,0:T(2,128)}, f32[2048]{0:T(1024)}, f32[2048]{0:T(1024)}) all-reduce(f32[2,2048]{1,0:T(2,128)S(1)} %pad_maximum_fusion.19, f32[2048]{0:T(1024)S(1)} %get-tuple-element.8, f32[2048]{0:T(1024)S(1)} %get-tuple-element.11), channel_id=1, replica_groups=mesh['dp'=8,'tp'=4] {'dp','tp'}, use_global_device_ids=true, to_apply=%region_8.9 | all-reduce | flops 8192 | bytes 65536 | tf_op jit(solution)/shard_map/psum | solution.py:91
  1233.7 313.0 %all-reduce.41.cloned.1.call-done = f32[1536,2048]{1,0:T(8,128)} async-done(((f32[1536,2048]{1,0:T(8,128)}), f32[1536,2048]{1,0:T(8,128)}) %all-reduce.41.cloned.1.call-update) | async-done | bytes 12582928 | tf_op jit(solution)/shard_map/psum | solution.py:90
  1546.7 11.5 copy.17
  (285 shorter events, 278.2 us)
Async XLA Ops:
  7.2 179.4 %copy-start = (f32[4,2048]{1,0:T(4,128)S(1)}, f32[4,2048]{1,0:T(4,128)}, u32[]{:S(2)}) copy-start(f32[4,2048]{1,0:T(4,128)} %param.10) | copy-start | bytes 98308
  7.2 159.9 %copy-start.20 = (f32[2048]{0:T(1024)S(1)}, f32[2048]{0:T(1024)}, u32[]{:S(2)}) copy-start(f32[2048]{0:T(1024)} %param.11) | copy-start | bytes 24580
  7.2 159.9 %copy-start.30 = (f32[2048]{0:T(1024)S(1)}, f32[2048]{0:T(1024)}, u32[]{:S(2)}) copy-start(f32[2048]{0:T(1024)} %param.12) | copy-start | bytes 24580
  7.2 159.9 %all-gather.2.cloned.1.call-start = ((), (), s32[]{:S(2)}) async-start(), calls=%async_computation.1 | async-start | bytes 31457280 | tf_op jit(solution)/shard_map/all_gather | solution.py:27
  8.0 1138.8 %reduce-scatter.2.cloned.1.call-start = ((), (), s32[]{:S(2)}) async-start(), calls=%async_computation.2 | async-start | bytes 62914560 | tf_op jit(solution)/shard_map/reduce_scatter | solution.py:71
  8.8 177.8 %copy-start.34 = (pred[512]{0:T(512)(128)(4,1)}, pred[512]{0:T(512)(128)(4,1)S(1)}, u32[]{:S(2)}) copy-start(pred[512]{0:T(512)(128)(4,1)S(1)} %pad_add_fusion.2) | copy-start | bytes 1540
  9.2 177.4 %copy-start.22 = (f32[512]{0:T(512)}, f32[512]{0:T(512)S(1)}, u32[]{:S(2)}) copy-start(f32[512]{0:T(512)S(1)} %broadcast_multiply_fusion.2) | copy-start | bytes 6148
  9.9 176.7 %copy-start.26 = (f32[512]{0:T(512)}, f32[512]{0:T(512)S(1)}, u32[]{:S(2)}) copy-start(f32[512]{0:T(512)S(1)} %add_rsqrt_fusion) | copy-start | bytes 6148
  355.5 7.0 copy-start.19
  379.4 9.8 copy-start.15
  393.9 4.0 copy-start.6
  393.9 4.0 copy-start.8
  394.0 4.9 copy-start.11
  436.0 6.9 copy-start.2
  436.0 6.9 copy-start.3
  436.0 8.0 copy-start.13
  436.0 8.0 copy-start.21
  436.0 8.0 copy-start.23
  436.0 8.0 copy-start.27
  436.0 8.0 copy-start.31
  634.8 17.5 %copy-start.18 = (f32[15,2048]{1,0:T(8,128)S(1)}, f32[15,2048]{1,0:T(8,128)}, u32[]{:S(2)}) copy-start(f32[15,2048]{1,0:T(8,128)} %slice.569) | copy-start | bytes 368644
  668.8 9.8 copy-start.16
  683.4 4.1 copy-start.7
  683.4 4.1 copy-start.9
  683.4 4.9 copy-start.12
  732.0 32.6 %copy-start.35 = (pred[512]{0:T(512)(128)(4,1)S(1)}, pred[512]{0:T(512)(128)(4,1)}, u32[]{:S(2)}) copy-start(pred[512]{0:T(512)(128)(4,1)} %copy-done.34) | copy-start | bytes 1540
  764.7 10.8 copy-start.32
  800.1 746.5 %all-reduce.41.cloned.1.call-start = ((), (), s32[]{:S(2)}) async-start(), calls=%async_computation.3 | async-start | bytes 25165824 | tf_op jit(solution)/shard_map/psum | solution.py:90
  1147.6 71.2 %copy-start.25 = (s32[1,512]{1,0:T(1,128)S(1)}, s32[1,512]{1,0:T(1,128)}, u32[]{:S(2)}) copy-start(s32[1,512]{1,0:T(1,128)} %param.9) | copy-start | bytes 6148
  1218.8 6.6 copy-start.14
  1218.8 6.6 copy-start.17
  1546.7 11.6 copy-start.1
  (7 other events, 11.8 us)
Sparse Core Ops, SparseCore 0:
  9.6 157.4 all-gather.1
  800.3 346.4 reduce-scatter.1
  1150.9 395.7 all-reduce.40
where the time goes:
time: 1590 us; the launch traced here: 1570 us
  waiting for transfers between devices  817 us (51%)
  local copies, waits for them, and re-layouts  495 us (31%)
  other arithmetic  102 us (6%)
  matrix products  92.1 us (6%)
  blocking collectives  43.3 us (3%)
    reduce_scatter x1, waiting for transfers between devices, local(): lax.psum_scatter(lax.dot_general(columns, normed_low, contract_first, pre...  347 us
    psum x1, waiting for transfers between devices, local(): weight_grad = lax.psum(weight_part, 'dp')  313 us
    slice x59, local copies, waits for them, and re-layouts, local(): lax.associative_scan(link, (next_decay, direct), reverse=True, axis=0)  214 us
    all_gather x1, waiting for transfers between devices, local(): lax.all_gather(weight, 'tp', axis=0, tiled=True)  157 us
    slice x53, local copies, waits for them, and re-layouts, local(): unused, cells = lax.associative_scan(link, (decay, drive), axis=0)  117 us
    pad x16, local copies, waits for them, and re-layouts, local(): lax.associative_scan(link, (next_decay, direct), reverse=True, axis=0)  54.8 us
    pad x16, local copies, waits for them, and re-layouts, local(): unused, cells = lax.associative_scan(link, (decay, drive), axis=0)  54.5 us
    psum x1, blocking collectives, local(): lax.psum((bias_part, gain_part, shift_part), ('dp', 'tp'))  43.3 us
  transfers between devices with their start and end apart: 3, of which 3 were waited for; matrix products, arithmetic and copies ran while one was open for 3% of the time, Pallas kernels for 0%

commit v1 on v0

--- a/solution.py
+++ b/solution.py
@@ -87,7 +87,7 @@
         )
         + outer
     )
-    weight_grad = lax.psum(weight_part, "dp")
+    weight_grad = jnp.sum(lax.all_gather(weight_part, "dp"), axis=0)
     bias_grad, gain_grad, shift_grad = lax.psum((bias_part, gain_part, shift_part), ("dp", "tp"))
     return (
         output,

time: 1590 us -> 3110 us (1.96)
  waiting for transfers between devices: 817 us -> 2210 us
  blocking collectives: 43.3 us -> 153 us
  other arithmetic: 102 us -> 138 us
    all_gather x0 -> x1, waiting for transfers between devices: none -> 1700 us  [local(): weight_grad = jnp.sum(lax.all_gather(weight_part, 'dp'), axis=0)]
    psum x1 -> x0, waiting for transfers between devices: 313 us -> none  [local(): weight_grad = lax.psum(weight_part, 'dp')]
    psum x1, blocking collectives: 43.3 us -> 153 us  [local(): lax.psum((bias_part, gain_part, shift_part), ('dp', 'tp'))]
    reduce_sum x0 -> x1, other arithmetic: none -> 36.2 us  [local(): weight_grad = jnp.sum(lax.all_gather(weight_part, 'dp'), axis=0)]
  transfers between devices with their start and end apart: 3 -> 3, of which waited for: 3 -> 3; matrix products, arithmetic and copies ran while one was open for 3% -> 1% of each run, Pallas kernels for 0% -> 0%
where the time goes in v1:
time: 3110 us; the launch traced here: 3090 us
  waiting for transfers between devices  2210 us (71%)
  local copies, waits for them, and re-layouts  483 us (16%)
  blocking collectives  153 us (5%)
  other arithmetic  138 us (4%)
  matrix products  92.4 us (3%)
    all_gather x1, waiting for transfers between devices, local(): weight_grad = jnp.sum(lax.all_gather(weight_part, 'dp'), axis=0)  1700 us
    reduce_scatter x1, waiting for transfers between devices, local(): lax.psum_scatter(lax.dot_general(columns, normed_low, contract_first, pre...  347 us
    slice x59, local copies, waits for them, and re-layouts, local(): lax.associative_scan(link, (next_decay, direct), reverse=True, axis=0)  214 us
    all_gather x1, waiting for transfers between devices, local(): lax.all_gather(weight, 'tp', axis=0, tiled=True)  157 us
    psum x1, blocking collectives, local(): lax.psum((bias_part, gain_part, shift_part), ('dp', 'tp'))  153 us
    slice x53, local copies, waits for them, and re-layouts, local(): unused, cells = lax.associative_scan(link, (decay, drive), axis=0)  117 us
  transfers between devices with their start and end apart: 3, of which 3 were waited for; matrix products, arithmetic and copies ran while one was open for 1% of the time, Pallas kernels for 0%

profile of v1, /device:TPU:0, one launch (start us, length us, event | category | flops | bytes accessed | tf_op | source)
XLA Modules:
  0.0 3088.7 jit_solution(3788173662014707168)
XLA Ops:
  10.5 156.7 %all-gather.4.cloned.1.call-done = bf16[6144,2048]{1,0:T(8,128)(2,1)} async-done(((bf16[1536,2048]{1,0:T(8,128)(2,1)}), bf16[6144,2048]{1,0:T(8,128)(2,1)}) %all-gather.4.cloned.1.call-update) | async-done | bytes 25165840 | tf_op jit(solution)/shard_map/all_gather | solution.py:27
  167.2 19.4 fusion
  195.2 9.8 slice.477
  205.0 9.8 slice.473
  214.8 10.1 slice.472
  229.8 9.8 slice.549
  239.6 9.8 slice.542
  249.4 9.8 slice.540
  260.1 10.0 slice.537
  270.1 9.8 slice.475
  280.0 9.8 slice.474
  403.0 16.5 pad.128
  419.4 16.7 pad.129
  453.3 9.8 slice.610
  463.2 9.8 slice.546
  473.0 9.9 slice.544
  482.8 16.7 slice.550
  499.6 16.7 slice.543
  516.3 16.6 slice.545
  532.9 16.7 slice.547
  617.9 17.0 slice.541
  634.9 17.1 slice.611
  692.3 16.5 pad.146
  708.8 16.5 pad.147
  731.8 32.6 %rev.2 = f32[512,2048]{1,0:T(8,128)} reverse(f32[512,2048]{1,0:T(8,128)} %add.366), dimensions={0} | reverse | bytes 8388608 | tf_op jit(solution)/shard_map/rev | solution.py:53
  764.4 10.8 fusion.71
  775.2 24.6 fusion.32
  799.9 346.6 %reduce-scatter.2.cloned.1.call-done = f32[1536,2048]{1,0:T(8,128)} async-done(((f32[6144,2048]{1,0:T(8,128)}), f32[1536,2048]{1,0:T(8,128)}) %reduce-scatter.2.cloned.1.call-update) | async-done | bytes 12582928 | tf_op jit(solution)/shard_map/reduce_scatter | solution.py:71
  1147.2 27.9 fusion.16
  1175.1 152.7 %all-reduce.38 = (f32[2,2048]{1,0:T(2,128)}, f32[2048]{0:T(1024)}, f32[2048]{0:T(1024)}) all-reduce(f32[2,2048]{1,0:T(2,128)S(1)} %pad_maximum_fusion.19, f32[2048]{0:T(1024)S(1)} %get-tuple-element.8, f32[2048]{0:T(1024)S(1)} %get-tuple-element.11), channel_id=1, replica_groups=mesh['dp'=8,'tp'=4] {'dp','tp'}, use_global_device_ids=true, to_apply=%region_8.9 | all-reduce | flops 8192 | bytes 65536 | tf_op jit(solution)/shard_map/psum | solution.py:91
  1342.8 1702.7 %all-gather.6.cloned.1.call-done = f32[12288,2048]{1,0:T(8,128)} async-done(((f32[1536,2048]{1,0:T(8,128)}), f32[12288,2048]{1,0:T(8,128)}) %all-gather.6.cloned.1.call-update) | async-done | bytes 100663312 | tf_op jit(solution)/shard_map/all_gather | solution.py:90
  3045.5 36.2 %reduce_sum.85 = f32[1536,2048]{1,0:T(8,128)} reduce(f32[8,1536,2048]{2,1,0:T(8,128)} %bitcast.3, f32[]{:T(128)} %constant.15.clone.1), dimensions={0}, to_apply=%region_5.6 | reduce | flops 22020096 | bytes 113246208 | tf_op jit(solution)/shard_map/reduce_sum | solution.py:90
  (285 shorter events, 278.2 us)
Async XLA Ops:
  7.2 179.4 %copy-start = (f32[4,2048]{1,0:T(4,128)S(1)}, f32[4,2048]{1,0:T(4,128)}, u32[]{:S(2)}) copy-start(f32[4,2048]{1,0:T(4,128)} %param.10) | copy-start | bytes 98308
  7.2 159.9 %copy-start.20 = (f32[2048]{0:T(1024)S(1)}, f32[2048]{0:T(1024)}, u32[]{:S(2)}) copy-start(f32[2048]{0:T(1024)} %param.11) | copy-start | bytes 24580
  7.2 159.9 %copy-start.30 = (f32[2048]{0:T(1024)S(1)}, f32[2048]{0:T(1024)}, u32[]{:S(2)}) copy-start(f32[2048]{0:T(1024)} %param.12) | copy-start | bytes 24580
  7.2 159.9 %all-gather.4.cloned.1.call-start = ((), (), s32[]{:S(2)}) async-start(), calls=%async_computation.1 | async-start | bytes 31457280 | tf_op jit(solution)/shard_map/all_gather | solution.py:27
  8.0 1138.5 %reduce-scatter.2.cloned.1.call-start = ((), (), s32[]{:S(2)}) async-start(), calls=%async_computation.2 | async-start | bytes 62914560 | tf_op jit(solution)/shard_map/reduce_scatter | solution.py:71
  8.8 177.8 %copy-start.34 = (pred[512]{0:T(512)(128)(4,1)}, pred[512]{0:T(512)(128)(4,1)S(1)}, u32[]{:S(2)}) copy-start(pred[512]{0:T(512)(128)(4,1)S(1)} %pad_add_fusion.2) | copy-start | bytes 1540
  9.2 177.4 %copy-start.22 = (f32[512]{0:T(512)}, f32[512]{0:T(512)S(1)}, u32[]{:S(2)}) copy-start(f32[512]{0:T(512)S(1)} %broadcast_multiply_fusion.2) | copy-start | bytes 6148
  9.9 176.7 %copy-start.26 = (f32[512]{0:T(512)}, f32[512]{0:T(512)S(1)}, u32[]{:S(2)}) copy-start(f32[512]{0:T(512)S(1)} %add_rsqrt_fusion) | copy-start | bytes 6148
  355.5 7.0 copy-start.19
  379.5 9.8 copy-start.15
  394.1 4.1 copy-start.6
  394.1 4.1 copy-start.8
  394.1 4.9 copy-start.11
  436.1 6.9 copy-start.2
  436.1 6.9 copy-start.3
  436.1 8.0 copy-start.13
  436.1 8.0 copy-start.21
  436.1 8.0 copy-start.23
  436.1 8.0 copy-start.27
  436.1 8.0 copy-start.31
  634.9 17.5 copy-start.18
  668.8 9.7 copy-start.16
  683.3 4.1 copy-start.7
  683.3 4.1 copy-start.9
  683.3 4.9 copy-start.12
  731.8 32.6 %copy-start.35 = (pred[512]{0:T(512)(128)(4,1)S(1)}, pred[512]{0:T(512)(128)(4,1)}, u32[]{:S(2)}) copy-start(pred[512]{0:T(512)(128)(4,1)} %copy-done.34) | copy-start | bytes 1540
  764.4 10.8 copy-start.32
  799.9 2245.7 %all-gather.6.cloned.1.call-start = ((), (), s32[]{:S(2)}) async-start(), calls=%async_computation.3 | async-start | bytes 113246208 | tf_op jit(solution)/shard_map/all_gather | solution.py:90
  1147.2 180.6 %copy-start.25 = (s32[1,512]{1,0:T(1,128)S(1)}, s32[1,512]{1,0:T(1,128)}, u32[]{:S(2)}) copy-start(s32[1,512]{1,0:T(1,128)} %param.9) | copy-start | bytes 6148
  1327.8 6.7 copy-start.14
  1327.8 6.7 copy-start.17
  3045.5 36.2 %copy-start.1 = (f32[4,2048]{1,0:T(4,128)S(1)}, f32[4,2048]{1,0:T(4,128)}, u32[]{:S(2)}) copy-start(f32[4,2048]{1,0:T(4,128)} %param.10) | copy-start | bytes 98308
  (7 other events, 11.5 us)
Sparse Core Ops, SparseCore 0:
  9.6 157.4 all-gather.3
  800.0 346.4 reduce-scatter.1
  1148.0 1897.4 all-gather.5
